TPU v7x, 512 devices: a whole 4x4x16 slice. The times are simulated.
512 devices in a mesh: rows: 128 (over x, z, core), cols: 4 (over y).
Axes of the slice: x: 4, y: 4, z: 16, core: 2. Of those that a mesh axis runs over, the one named last changes fastest.
Arguments:
- tiles: bfloat16 [65536, 4096], P(('rows', 'cols')), may hold values from -0.125 to 0.125
- integral_cd_tile: int32 [65536], P(('rows', 'cols')), may hold values from 0 to 511
- part_dest: int32 [16384, 1], P(('rows', 'cols')), may hold values from 0 to 127; in each aligned block of 32 rows (0 to 31, 32 to 63, ...) at most 2 rows name the same one
- partial_row_place: int32 [16384], P(('rows', 'cols')), may hold values from 0 to 15
- amplitudes: bfloat16 [4, 512, 4096], P('cols', 'rows'), may hold values from -6 to 6
- residual_in: float32 [128, 16, 4096], P('rows', 'cols'), may hold values from -6 to 6
Outputs:
- residual: float32 [128, 16, 4096], P('rows', 'cols')
Inputs may be any that keep to these rules, and one draw needn't show every extreme that they name: `part_dest`: among the 32 partial tiles of one device no index of rows is named more than 2 times, and at least one is named exactly 2 times.
All inputs are finite; a program needn't handle non-finite values.
Results may differ from a plain program's by a relative error of at most 0.0022.
Values may be sent and summed in bfloat16 or wider, within the bound.
A program may use at most 64 MiB of HBM per device.

v0:
```python
import jax
import jax.numpy as jnp
from jax import lax
from jax.sharding import PartitionSpec as P

TILE_SPAN = 64
NIJ = 64
TILES_PER_PART = 4
PAB = 32
OWNR = 16


def per_device(tiles, integral_cd_tile, part_dest, partial_row_place, amplitudes, residual_in):
    gathered = lax.all_gather(amplitudes, "rows", axis=1, tiled=True)[0]
    picked = jnp.take(gathered, integral_cd_tile, axis=0).reshape(
        PAB, TILES_PER_PART, NIJ, TILE_SPAN
    )
    block_list = tiles.reshape(PAB, TILES_PER_PART, TILE_SPAN, TILE_SPAN)
    per_tile = jnp.einsum("ptic,ptac->ptia", picked, block_list, preferred_element_type=jnp.float32)
    partial_value = jnp.sum(per_tile, axis=1)
    partial_value = partial_value.reshape(PAB, NIJ * TILE_SPAN).astype(jnp.bfloat16)
    row_count = lax.axis_size("rows")
    capacity = max(2, 2 * PAB // row_count)
    destination = part_dest[:, 0]
    onehot = (destination[:, None] == jnp.arange(row_count, dtype=jnp.int32)[None, :]).astype(
        jnp.int32
    )
    earlier = jnp.sum((jnp.cumsum(onehot, axis=0) - onehot) * onehot, axis=1)
    position = destination * capacity + earlier
    outgoing = (
        jnp.zeros((row_count * capacity, NIJ * TILE_SPAN), jnp.bfloat16)
        .at[position]
        .set(partial_value)
    )
    slot_ids = (
        jnp.full((row_count * capacity,), float(OWNR), jnp.float32)
        .at[position]
        .set(partial_row_place.astype(jnp.float32))
        .astype(jnp.bfloat16)
    )
    incoming, incoming_ids = (
        lax.all_to_all(
            outgoing.reshape(row_count, capacity, NIJ * TILE_SPAN),
            "rows",
            split_axis=0,
            concat_axis=0,
            tiled=True,
        ),
        lax.all_to_all(
            slot_ids.reshape(row_count, capacity), "rows", split_axis=0, concat_axis=0, tiled=True
        ),
    )
    incoming = incoming.reshape(row_count * capacity, NIJ * TILE_SPAN)
    incoming_ids = incoming_ids.reshape(row_count * capacity).astype(jnp.float32)
    select = (incoming_ids[None, :] == jnp.arange(OWNR, dtype=jnp.float32)[:, None]).astype(
        jnp.bfloat16
    )
    owned = jnp.dot(select, incoming, preferred_element_type=jnp.float32)
    shared = lax.psum_scatter(owned, "cols", scatter_dimension=0, tiled=True)
    return residual_in + shared[None, :, :]


def solution(mesh):
    return jax.shard_map(
        per_device,
        mesh=mesh,
        in_specs=(
            P(("rows", "cols"), None),
            P(("rows", "cols")),
            P(("rows", "cols"), None),
            P(("rows", "cols")),
            P("cols", "rows", None),
            P("rows", "cols", None),
        ),
        out_specs=P("rows", "cols", None),
        check_vma=False,
    )
```

profile of v0, /device:TPU:6, one launch (start us, length us, event | category | flops | bytes accessed | tf_op | source)
XLA Modules:
  0.0 361.5 jit_solution(1006233409174559257)
XLA Ops:
  6.5 1.4 copy.10
  8.0 0.7 convert_element_type.27
  8.7 0.7 fusion.13
  9.5 0.8 select_reduce_fusion
  10.3 0.7 fusion.16
  11.0 0.7 scatter_custom_fusion
  11.6 0.8 all_to_all.12
  12.4 19.9 %all-to-all-start = ((bf16[128,1,2]{2,1,0:T(2,128)(2,1)}), bf16[128,1,2]{2,1,0:T(2,128)(2,1)S(1)}, u32[]{:S(2)}, u32[]{:S(2)}) async-start(bf16[128,1,2]{2,1,0:T(2,128)(2,1)} %all_to_all.12), calls=%async_computation | async-start | bytes 131072 | tf_op jit(solution)/shard_map/all_to_all | solution.py:49
  32.4 3.3 reshape.37
  35.8 124.4 %all-gather.2.cloned.1.call-done = bf16[1,512,4096]{2,0,1:T(2,128)(2,1)} async-done(((bf16[1,4,4096]{2,0,1:T(2,128)(2,1)}), bf16[1,512,4096]{2,0,1:T(2,128)(2,1)}) %all-gather.2.cloned.1.call-update) | async-done | bytes 4194320 | tf_op jit(solution)/shard_map/all_gather | solution.py:14
  160.2 10.1 %copy.14 = bf16[1,512,4096]{2,1,0:T(8,128)(2,1)} copy(bf16[1,512,4096]{2,0,1:T(2,128)(2,1)} %all-gather.2.cloned.1.call-done) | data formatting | bytes 8388608
  170.3 4.9 %gather_fusion = bf16[128,4096]{1,0:T(8,128)(2,1)S(1)} fusion(bf16[512,4096]{1,0:T(8,128)(2,1)} %bitcast.22, s32[1024]{0:T(1024)S(1)} %pad_clamp_fusion), kind=kCustom, calls=%fused_computation | custom fusion | bytes 2097664 | tf_op jit(solution)/shard_map/jit(_take)/gather | solution.py:15
  175.3 3.3 gather.7
  178.6 2.3 fusion.6
  180.9 0.5 reshape.61
  181.4 2.0 scatter_custom_fusion.1
  183.4 2.7 reshape.38
  186.1 12.7 %all-to-all-start.1 = ((bf16[128,2,4096]{2,1,0:T(2,128)(2,1)}), bf16[128,2,4096]{2,1,0:T(2,128)(2,1)S(1)}, u32[]{:S(2)}, u32[]{:S(2)}) async-start(bf16[128,2,4096]{2,1,0:T(2,128)(2,1)} %reshape.38), calls=%async_computation.1 | async-start | bytes 4194304 | tf_op jit(solution)/shard_map/all_to_all | solution.py:42
  199.1 97.1 %all-to-all-done.1 = bf16[128,2,4096]{2,1,0:T(2,128)(2,1)S(1)} async-done(((bf16[128,2,4096]{2,1,0:T(2,128)(2,1)}), bf16[128,2,4096]{2,1,0:T(2,128)(2,1)S(1)}, u32[]{:S(2)}, u32[]{:S(2)}) %all-to-all-start.1) | async-done | bytes 2097184 | tf_op jit(solution)/shard_map/all_to_all | solution.py:42
  296.2 2.2 reshape.39
  298.4 2.7 fusion.14
  301.2 1.3 dynamic-slice
  303.1 50.0 %all-reduce.3.cloned.1.call-done = f32[16,4096]{1,0:T(8,128)} async-done(((f32[16,4096]{1,0:T(8,128)}), f32[16,4096]{1,0:T(8,128)}) %all-reduce.3.cloned.1.call-update) | async-done | bytes 262160
  353.2 1.6 fusion.12
  (17 shorter events, 0.6 us)
Async XLA Ops:
  6.5 29.1 %copy-start.1 = (s32[128]{0:T(128)S(1)}, s32[128]{0:T(128)}, u32[]{:S(2)}) copy-start(s32[128]{0:T(128)} %param.7) | copy-start | bytes 1540
  6.5 153.7 %all-gather.2.cloned.1.call-start = ((), (), s32[]{:S(2)}) async-start(), calls=%async_computation.2 | async-start | bytes 8454144 | tf_op jit(solution)/shard_map/all_gather | solution.py:14
  12.4 173.6 %all-to-all-start = ((bf16[128,1,2]{2,1,0:T(2,128)(2,1)}), bf16[128,1,2]{2,1,0:T(2,128)(2,1)S(1)}, u32[]{:S(2)}, u32[]{:S(2)}) async-start(bf16[128,1,2]{2,1,0:T(2,128)(2,1)} %all_to_all.12), calls=%async_computation | async-start | bytes 131072 | tf_op jit(solution)/shard_map/all_to_all | solution.py:49
  186.1 110.2 %all-to-all-start.1 = ((bf16[128,2,4096]{2,1,0:T(2,128)(2,1)}), bf16[128,2,4096]{2,1,0:T(2,128)(2,1)S(1)}, u32[]{:S(2)}, u32[]{:S(2)}) async-start(bf16[128,2,4096]{2,1,0:T(2,128)(2,1)} %reshape.38), calls=%async_computation.1 | async-start | bytes 4194304 | tf_op jit(solution)/shard_map/all_to_all | solution.py:42
  198.7 154.4 %all-reduce.3.cloned.1.call-start = ((), (), s32[]{:S(2)}) async-start(), calls=%async_computation.3 | async-start | bytes 524288
  298.4 54.7 %copy-start = (f32[1,4,4096]{2,1,0:T(4,128)S(1)}, f32[1,4,4096]{2,1,0:T(4,128)}, u32[]{:S(2)}) copy-start(f32[1,4,4096]{2,1,0:T(4,128)} %param.11) | copy-start | bytes 196612
Sparse Core Ops, SparseCore 0:
  10.5 149.6 all-gather.1
  301.3 51.7 all-reduce.2
where the time goes:
time: 362 us
  waiting for transfers between devices  272 us (75%)
  local copies, waits for them, and re-layouts  33.4 us (9%)
  starting transfers between devices  32.6 us (9%)
  between operations  14.2 us (4%)
  matrix products  5.08 us (1%)
  other arithmetic  4.7 us (1%)
    all_gather x1, waiting for transfers between devices, per_device(): gathered = lax.all_gather(amplitudes, 'rows', axis=1, tiled=True)[0]  124 us
    all_to_all x1, waiting for transfers between devices, per_device(): lax.all_to_all(outgoing.reshape(row_count, capacity, NIJ * TILE_SPAN), 'r...  97.1 us
    unnamed x3, waiting for transfers between devices  50.1 us
    all_to_all x1, starting transfers between devices, per_device(): lax.all_to_all(slot_ids.reshape(row_count, capacity), 'rows', split_axis=...  19.9 us
    unnamed x7, local copies, waits for them, and re-layouts  12.8 us
    all_to_all x1, starting transfers between devices, per_device(): lax.all_to_all(outgoing.reshape(row_count, capacity, NIJ * TILE_SPAN), 'r...  12.7 us
    gather x2, local copies, waits for them, and re-layouts, per_device(): jnp.take(gathered, integral_cd_tile, axis=0)  8.25 us
  transfers between devices with their start and end apart: 4, of which 3 were waited for; matrix products, arithmetic and copies ran while one was open for 10% of the time, Pallas kernels for 0%

commit v1 on v0

v1 whole, which is shorter than its diff:
```python
import jax
import jax.numpy as jnp
from jax import lax
from jax.experimental import pallas as pl
from jax.experimental.pallas import tpu as pltpu
from jax.sharding import PartitionSpec as P

PAB = 32
HALF = 2048
MESH = pl.DeviceIdType.MESH


def coords():
    r = lax.axis_index("rows")
    y = lax.axis_index("cols")
    return r // 32, y, lax.rem(r // 2, 16), lax.rem(r, 2)


def dev(x, y, z, c):
    return ((lax.rem(x + 4, 4) * 16 + lax.rem(z + 16, 16)) * 2 + lax.rem(c, 2), lax.rem(y + 4, 4))


def ladder_kernel(
    cd_ref, codes_ref, amp_ref, tiles_ref, out_ref,
    amp, tv, tsc, wbuf, osc, xa, xb, ca, cb, sa, sb, ra, rb, se, re, sf, rf,
    tile_sem, z_s, z_r, x_s, x_r, k_s, k_r, c_s, c_r, p_s, p_r, q_s, q_r, e_s, e_r, f_s, f_r,
):
    x, y, z, c = coords()
    sent = []

    def send(src, dst, ss, rs, to):
        cp = pltpu.make_async_remote_copy(
            src_ref=src, dst_ref=dst, send_sem=ss, recv_sem=rs, device_id=to, device_id_type=MESH
        )
        cp.start()
        sent.append(cp)

    def arrived(dst, rs, to):
        pltpu.make_async_remote_copy(
            src_ref=dst, dst_ref=dst, send_sem=rs, recv_sem=rs, device_id=to, device_id_type=MESH
        ).wait_recv()

    tiles_in = pltpu.make_async_copy(tiles_ref, tv, tile_sem)
    tiles_in.start()
    sib = dev(x, y, z, c + 1)

    def spot(cc, xx, slot):
        return pl.multiple_of(((cc * 4 + xx) * 16 + slot) * 4, 4)

    def block(xx, slot, n=1, cc=None):
        return amp.at[pl.ds(spot(c if cc is None else cc, xx, slot), 4 * n)]

    amp[pl.ds(spot(c, x, 8), 4)] = amp_ref[...]
    ca[y * 2 + c] = codes_ref[...]
    cb[x * 2 + c] = codes_ref[...]

    barrier = pltpu.get_barrier_semaphore()
    friends = [dev(x, y, z + d, c) for d in (1, -1, 2, -2, 3, -3, 4, -4, 8)]
    friends += [dev(x + d, y, z, c) for d in (1, 2, 3)]
    friends += [dev(x, y + d, z, c) for d in (1, 2, 3)]
    friends += [sib]
    for t in friends:
        pl.semaphore_signal(barrier, inc=1, device_id=t, device_id_type=MESH)
    pl.semaphore_wait(barrier, len(friends))

    def z_send(slot, step):
        nslot = slot - step
        send(block(x, slot), block(x, nslot), z_s.at[nslot], z_r.at[nslot], dev(x, y, z + step, c))

    def z_wait(slot):
        arrived(block(x, slot), z_r.at[slot], sib)

    def x_send(g, slot, n):
        for i in (1, 2, 3):
            send(block(x, slot, n), block(x, slot, n), x_s.at[g, i - 1], x_r.at[g, i - 1], dev(x + i, y, z, c))

    def x_wait(g, slot, n):
        for i in (1, 2, 3):
            arrived(block(lax.rem(x + 4 - i, 4), slot, n), x_r.at[g, i - 1], sib)

    def k_send(g, slot, n):
        for i in range(4):
            xs = lax.rem(x + 4 - i, 4)
            send(block(xs, slot, n), block(xs, slot, n), k_s.at[g, i], k_r.at[g, i], sib)

    def k_wait(g, slot, n):
        for i in range(4):
            xs = lax.rem(x + 4 - i, 4)
            arrived(block(xs, slot, n, 1 - c), k_r.at[g, i], sib)

    for step in (2, -2, 1, -1):
        z_send(8, step)
    x_send(0, 8, 1)
    for i in (1, 2, 3):
        me = ca.at[y * 2 + c]
        send(me, me, c_s.at[0, i - 1], c_r.at[0, i - 1], dev(x, y + i, z, c))
        me = cb.at[x * 2 + c]
        send(me, me, c_s.at[1, i - 1], c_r.at[1, i - 1], dev(x + i, y, z, c))

    rows = lax.broadcasted_iota(jnp.int32, (128, 64), 0)
    cols = lax.broadcasted_iota(jnp.int32, (128, 64), 1)
    par = rows // 64
    ab = lax.rem(rows, 64)
    take = (cols == ab // 2 + 32 * (lax.rem(ab, 2) ^ par)).astype(jnp.bfloat16)
    keep = lax.rem(lax.broadcasted_iota(jnp.int32, (128, 512), 1), 128) // 64 == (
        lax.broadcasted_iota(jnp.int32, (128, 512), 0) // 64
    )

    def relayout(j, carry):
        base = pl.multiple_of(j * 16, 16)
        v = tv[pl.ds(base, 16), :].astype(jnp.float32)
        for l in range(32):
            tsc[pl.ds(base * 32 + l, 16, stride=32), :] = v[:, l * 128 : (l + 1) * 128]
        return carry

    def build(q, carry):
        both = []
        for t in range(4):
            b2 = tsc[pl.ds(pl.multiple_of((q * 4 + t) * 32, 32), 32), :]
            both.append(jnp.concatenate([b2, pltpu.roll(b2, 64, 1)], axis=0))
        r = jnp.concatenate(both, axis=1).astype(jnp.bfloat16)
        g = jnp.dot(take, r, preferred_element_type=jnp.float32)
        wbuf[q] = jnp.where(keep, g, 0.0).astype(jnp.bfloat16)
        return carry

    def prep(lo, hi):
        lax.fori_loop(lo // 4, hi // 4, relayout, 0)
        lax.fori_loop(lo, hi, build, 0)

    tiles_in.wait()
    prep(0, 4)
    z_wait(6)
    z_send(6, 2)
    z_send(6, 1)
    z_wait(10)
    z_send(10, -2)
    z_send(10, -1)
    z_wait(7)
    x_send(1, 6, 2)
    z_wait(9)
    x_send(2, 9, 2)
    prep(4, 8)
    z_wait(4)
    z_send(4, 2)
    z_send(4, 1)
    z_wait(12)
    z_send(12, -2)
    z_send(12, -1)
    z_wait(5)
    x_send(3, 4, 2)
    z_wait(11)
    x_send(4, 11, 2)
    prep(8, 16)
    z_wait(2)
    z_send(2, 2)
    z_send(2, 1)
    z_wait(14)
    z_send(14, -1)
    z_wait(3)
    x_send(5, 2, 2)
    z_wait(13)
    x_send(6, 13, 2)
    x_wait(0, 8, 1)
    x_wait(1, 6, 2)
    x_wait(2, 9, 2)
    x_wait(3, 4, 2)
    x_wait(4, 11, 2)
    k_send(0, 4, 9)
    for i in (1, 2, 3):
        arrived(ca.at[lax.rem(y + 4 - i, 4) * 2 + c], c_r.at[0, i - 1], sib)
        arrived(cb.at[lax.rem(x + 4 - i, 4) * 2 + c], c_r.at[1, i - 1], sib)
    for i in range(4):
        s = ca.at[lax.rem(y + 4 - i, 4) * 2 + c]
        send(s, s, c_s.at[0, 3 + i], c_r.at[0, 3 + i], sib)
        s = cb.at[lax.rem(x + 4 - i, 4) * 2 + c]
        send(s, s, c_s.at[1, 3 + i], c_r.at[1, 3 + i], sib)
    prep(16, 32)
    z_wait(0)
    z_wait(1)
    x_send(7, 0, 2)
    z_wait(15)
    x_send(8, 15, 1)
    x_wait(5, 2, 2)
    x_wait(7, 0, 2)
    k_send(1, 0, 4)
    x_wait(6, 13, 2)
    x_wait(8, 15, 1)
    k_send(2, 13, 3)
    for i in range(4):
        arrived(ca.at[lax.rem(y + 4 - i, 4) * 2 + 1 - c], c_r.at[0, 3 + i], sib)
        arrived(cb.at[lax.rem(x + 4 - i, 4) * 2 + 1 - c], c_r.at[1, 3 + i], sib)

    d = lax.broadcasted_iota(jnp.int32, (256, 256), 0)
    other = d // 64
    zz = lax.rem(d // 4, 4) * 4 + lax.rem(d // 16, 4)
    p = lax.rem(d, 4)
    lane = lax.broadcasted_iota(jnp.int32, (1, 128), 1) // 32

    def spread(ref):
        parts = []
        for h in range(2):
            row = ref[4 * h][0:1, :]
            for j in (1, 2, 3):
                row = jnp.where(lane == j, ref[4 * h + j][0:1, :], row)
            parts.append(row)
        return jnp.concatenate(parts, axis=1)

    want_a = ((other * 16 + zz) * 2 + c) * 16 + y * 4 + p
    sel_a = (spread(ca) == want_a).astype(jnp.bfloat16)
    want_b = ((x * 16 + zz) * 2 + c) * 16 + other * 4 + p
    sel_b = (spread(cb) == want_b).astype(jnp.bfloat16)

    k_wait(0, 4, 9)
    k_wait(1, 0, 4)
    k_wait(2, 13, 3)

    def product(q, carry):
        parts = []
        for t in range(4):
            cd = cd_ref[q * 4 + t]
            hr = cd // 4
            slot = lax.rem(lax.rem(hr // 2, 16) - z + 24, 16)
            parts.append(amp[((lax.rem(hr, 2) * 4 + hr // 32) * 16 + slot) * 4 + lax.rem(cd, 4)])
        a = jnp.concatenate(parts, axis=1)
        o = lax.dot_general(a, wbuf[q], (((1,), (1,)), ((), ())), preferred_element_type=jnp.float32)
        osc[pl.ds(pl.multiple_of(q * 32, 32), 32), :] = o
        return carry

    lax.fori_loop(0, PAB, product, 0)
    mine_a = xa.at[y * 2 + c]
    mine_b = xb.at[x * 2 + c]
    for r in range(16):
        mine_a[:, r * 128 : (r + 1) * 128] = osc[pl.ds(r, PAB, stride=32), :].astype(jnp.bfloat16)
    for i in (1, 2, 3):
        send(mine_a, mine_a, p_s.at[0, i - 1], p_r.at[0, i - 1], dev(x, y + i, z, c))
    for r in range(16):
        mine_b[:, r * 128 : (r + 1) * 128] = osc[pl.ds(16 + r, PAB, stride=32), :].astype(jnp.bfloat16)
    for i in (1, 2, 3):
        send(mine_b, mine_b, p_s.at[1, i - 1], p_r.at[1, i - 1], dev(x + i, y, z, c))

    for i in range(4):
        for h, (ref, me) in enumerate(((xa, y), (xb, x))):
            s = ref.at[lax.rem(me + 4 - i, 4) * 2 + c]
            if i > 0:
                arrived(s, p_r.at[h, i - 1], sib)
            send(s, s, p_s.at[h, 3 + i], p_r.at[h, 3 + i], sib)

    def dense(sel, src, dst):
        def chunk(n, carry):
            lanes = pl.ds(pl.multiple_of(n * 256, 256), 256)
            v = src[:, :, lanes].reshape(256, 256)
            s = jnp.dot(sel, v, preferred_element_type=jnp.float32).astype(jnp.bfloat16)
            dst[:, :, lanes] = s.reshape(4, 64, 256)
            return carry

        lax.fori_loop(0, HALF // 256, chunk, 0)

    for i in range(4):
        arrived(xa.at[lax.rem(y + 4 - i, 4) * 2 + 1 - c], p_r.at[0, 3 + i], sib)
    dense(sel_a, xa, sa)
    for i in (1, 2, 3):
        send(sa.at[lax.rem(x + i, 4)], ra.at[i - 1], q_s.at[0, i - 1], q_r.at[0, i - 1], dev(x + i, y, z, c))
    for i in range(4):
        arrived(xb.at[lax.rem(x + 4 - i, 4) * 2 + 1 - c], p_r.at[1, 3 + i], sib)
    dense(sel_b, xb, sb)
    for i in (1, 2, 3):
        send(sb.at[lax.rem(y + i, 4)], rb.at[i - 1], q_s.at[1, i - 1], q_r.at[1, i - 1], dev(x, y + i, z, c))

    def gathered(own, got, dst, at):
        def chunk(n, carry):
            lanes = pl.ds(pl.multiple_of(n * 256, 256), 256)
            s = own[:, lanes].astype(jnp.float32)
            for i in range(3):
                s = s + got[i, :, lanes].astype(jnp.float32)
            dst[:, :, pl.ds(pl.multiple_of(at + n * 256, 256), 256)] = s.astype(jnp.bfloat16).reshape(4, 16, 256)
            return carry

        lax.fori_loop(0, HALF // 256, chunk, 0)

    for i in (1, 2, 3):
        arrived(ra.at[i - 1], q_r.at[0, i - 1], sib)
    gathered(sa.at[x], ra, se, 0)
    for i in (1, 2, 3):
        arrived(rb.at[i - 1], q_r.at[1, i - 1], sib)
    gathered(sb.at[y], rb, se, HALF)

    a4 = z // 4
    b4 = lax.rem(z, 4)
    for i in (1, 2, 3):
        to = lax.rem(b4 + i, 4)
        send(se.at[to], re.at[i - 1], e_s.at[i - 1], e_r.at[i - 1], dev(x, y, a4 * 4 + to, c))
    for i in (1, 2, 3):
        arrived(re.at[i - 1], e_r.at[i - 1], sib)
    for u in range(4):
        lanes = slice(u * 1024, (u + 1) * 1024)
        s = se[b4, :, lanes].astype(jnp.float32)
        for i in range(3):
            s = s + re[i, :, lanes].astype(jnp.float32)
        for k in range(4):
            sf[k, u] = s[k * 4 : (k + 1) * 4, :]
    for i in (1, 2, 3):
        to = lax.rem(a4 + i, 4)
        send(sf.at[to], rf.at[i - 1], f_s.at[i - 1], f_r.at[i - 1], dev(x, y, to * 4 + b4, c))
    for i in (1, 2, 3):
        arrived(rf.at[i - 1], f_r.at[i - 1], sib)
    for u in range(4):
        out_ref[:, u * 1024 : (u + 1) * 1024] = sf[a4, u] + rf[0, u] + rf[1, u] + rf[2, u]

    for cp in sent:
        cp.wait_send()


def per_device(tiles, integral_cd_tile, part_dest, partial_row_place, amplitudes, residual_in):
    codes = jnp.tile((part_dest[:, 0] * 16 + partial_row_place)[None, :], (8, 4))
    bf16, f32, dma = jnp.bfloat16, jnp.float32, pltpu.SemaphoreType.DMA
    vmem = pl.BlockSpec(memory_space=pltpu.VMEM)
    ladder = pl.pallas_call(
        ladder_kernel,
        out_shape=jax.ShapeDtypeStruct((4, 4096), f32),
        in_specs=[
            pl.BlockSpec(memory_space=pltpu.SMEM),
            vmem,
            vmem,
            pl.BlockSpec(memory_space=pl.ANY),
        ],
        out_specs=vmem,
        scratch_shapes=[
            pltpu.VMEM((512, 32, 128), bf16),
            pltpu.VMEM((128, 4096), bf16),
            pltpu.VMEM((4096, 128), f32),
            pltpu.VMEM((32, 128, 512), bf16),
            pltpu.VMEM((1024, 128), f32),
            pltpu.VMEM((8, 32, HALF), bf16),
            pltpu.VMEM((8, 32, HALF), bf16),
            pltpu.VMEM((8, 8, 128), jnp.int32),
            pltpu.VMEM((8, 8, 128), jnp.int32),
            pltpu.VMEM((4, 64, HALF), bf16),
            pltpu.VMEM((4, 64, HALF), bf16),
            pltpu.VMEM((3, 64, HALF), bf16),
            pltpu.VMEM((3, 64, HALF), bf16),
            pltpu.VMEM((4, 16, 4096), bf16),
            pltpu.VMEM((3, 16, 4096), bf16),
            pltpu.VMEM((4, 4, 4, 1024), f32),
            pltpu.VMEM((3, 4, 4, 1024), f32),
            dma,
            dma((16,)), dma((16,)),
            dma((9, 3)), dma((9, 3)),
            dma((3, 4)), dma((3, 4)),
            dma((2, 7)), dma((2, 7)),
            dma((2, 7)), dma((2, 7)),
            dma((2, 3)), dma((2, 3)),
            dma((3,)), dma((3,)),
            dma((3,)), dma((3,)),
        ],
        compiler_params=pltpu.CompilerParams(
            collective_id=0, has_side_effects=True, vmem_limit_bytes=48 << 20
        ),
    )(integral_cd_tile, codes, amplitudes.reshape(4, 32, 128), tiles)
    return residual_in + ladder[None]


def solution(mesh):
    return jax.shard_map(
        per_device,
        mesh=mesh,
        in_specs=(
            P(("rows", "cols"), None),
            P(("rows", "cols")),
            P(("rows", "cols"), None),
            P(("rows", "cols")),
            P("cols", "rows", None),
            P("rows", "cols", None),
        ),
        out_specs=P("rows", "cols", None),
        check_vma=False,
    )
```

time: 362 us -> 113 us (0.31)
  the two profiles are of different devices: /device:TPU:6 before, /device:TPU:96 now
where the time goes in v1:
time: 113 us
  Pallas kernels  109 us (96%)
  local copies, waits for them, and re-layouts  3.41 us (3%)
    pallas_call x1, Pallas kernels, per_device(): pl.pallas_call(ladder_kernel, out_shape=jax.ShapeDtypeStruct((4, 4096), f...  109 us
    unnamed x11, local copies, waits for them, and re-layouts  3.32 us

profile of v1, /device:TPU:96, one launch (start us, length us, event | category | flops | bytes accessed | tf_op | source)
XLA Modules:
  0.0 112.8 jit_solution(7604083866647215116)
XLA Ops:
  0.0 0.0 copy-start.3
  0.0 0.0 copy-start.4
  0.0 0.7 copy-done.3
  0.7 0.0 copy-done.4
  0.7 0.1 tile.11
  0.8 0.8 copy.9
  1.5 0.0 copy-start.1
  1.5 0.7 copy-done.1
  2.2 0.0 copy-start
  2.2 1.2 %copy-done = bf16[128,4096]{1,0:T(8,128)(2,1)S(1)} copy-done((bf16[128,4096]{1,0:T(8,128)(2,1)S(1)}, bf16[128,4096]{1,0:T(8,128)(2,1)}, u32[]{:S(2)}) %copy-start) | copy-done | bytes 1048600
  3.4 0.0 copy-start.2
  3.4 108.7 %shard_map.64 = f32[4,4096]{1,0:T(4,128)S(1)} custom-call(s32[128]{0:T(128)S(1)} %copy-done.1, s32[8,128]{1,0:T(8,128)S(1)} %tile.12.codes_ref, bf16[4,32,128]{2,1,0:T(8,128)(2,1)S(1)} %bitcast.9, bf16[128,4096]{1,0:T(8,128)(2,1)S(1)} %copy-done), custom_call_target="tpu_custom_call" | custom-call | tf_op jit(solution)/shard_map/pallas_call | solution.py:317
  112.2 0.0 copy-done.2
  112.2 0.6 bitcast_add_fusion
  (3 shorter events, 0.0 us)
Async XLA Ops:
  0.0 0.7 copy-start.3
  0.0 0.7 copy-start.4
  1.5 0.7 copy-start.1
  2.2 1.2 %copy-start = (bf16[128,4096]{1,0:T(8,128)(2,1)S(1)}, bf16[128,4096]{1,0:T(8,128)(2,1)}, u32[]{:S(2)}) copy-start(bf16[128,4096]{1,0:T(8,128)(2,1)} %tiles_ref.1) | copy-start | bytes 3145732
  3.4 108.7 %copy-start.2 = (f32[1,4,4096]{2,1,0:T(4,128)S(1)}, f32[1,4,4096]{2,1,0:T(4,128)}, u32[]{:S(2)}) copy-start(f32[1,4,4096]{2,1,0:T(4,128)} %param.11) | copy-start | bytes 196612

commit v2 on v1

--- a/solution.py
+++ b/solution.py
@@ -21,9 +21,9 @@
 
 
 def ladder_kernel(
-    cd_ref, codes_ref, amp_ref, tiles_ref, out_ref,
-    amp, tv, tsc, wbuf, osc, xa, xb, ca, cb, sa, sb, ra, rb, se, re, sf, rf,
-    tile_sem, z_s, z_r, x_s, x_r, k_s, k_r, c_s, c_r, p_s, p_r, q_s, q_r, e_s, e_r, f_s, f_r,
+    cd_hbm, dest_hbm, place_hbm, amp_hbm, tiles_hbm, out_ref,
+    cd_ref, dest, place, amp4, amp, tv, tsc, wbuf, osc, xa, xb, ca, cb, sa, sb, ra, rb, se, re, sf, rf,
+    in_sem, z_s, z_r, x_s, x_r, k_s, k_r, c_s, c_r, p_s, p_r, q_s, q_r, e_s, e_r, f_s, f_r,
 ):
     x, y, z, c = coords()
     sent = []
@@ -40,27 +40,37 @@
             src_ref=dst, dst_ref=dst, send_sem=rs, recv_sem=rs, device_id=to, device_id_type=MESH
         ).wait_recv()
 
-    tiles_in = pltpu.make_async_copy(tiles_ref, tv, tile_sem)
-    tiles_in.start()
     sib = dev(x, y, z, c + 1)
-
-    def spot(cc, xx, slot):
-        return pl.multiple_of(((cc * 4 + xx) * 16 + slot) * 4, 4)
-
-    def block(xx, slot, n=1, cc=None):
-        return amp.at[pl.ds(spot(c if cc is None else cc, xx, slot), 4 * n)]
-
-    amp[pl.ds(spot(c, x, 8), 4)] = amp_ref[...]
-    ca[y * 2 + c] = codes_ref[...]
-    cb[x * 2 + c] = codes_ref[...]
-
     barrier = pltpu.get_barrier_semaphore()
-    friends = [dev(x, y, z + d, c) for d in (1, -1, 2, -2, 3, -3, 4, -4, 8)]
+    friends = [dev(x, y, z + d, c) for d in (1, -1, 2, -2, 4, -4, 8)]
     friends += [dev(x + d, y, z, c) for d in (1, 2, 3)]
     friends += [dev(x, y + d, z, c) for d in (1, 2, 3)]
     friends += [sib]
     for t in friends:
         pl.semaphore_signal(barrier, inc=1, device_id=t, device_id_type=MESH)
+    loads = []
+    for i, (src, dst) in enumerate(
+        ((amp_hbm, amp4), (dest_hbm, dest), (place_hbm, place), (cd_hbm, cd_ref), (tiles_hbm, tv))
+    ):
+        loads.append(pltpu.make_async_copy(src, dst, in_sem.at[i]))
+        loads[-1].start()
+
+    def spot(cc, xx, slot):
+        return pl.multiple_of(((cc * 4 + xx) * 16 + slot) * 4, 4)
+
+    def block(xx, slot, n=1, cc=None):
+        return amp.at[pl.ds(spot(c if cc is None else cc, xx, slot), 4 * n)]
+
+    for i in range(3):
+        loads[i].wait()
+    v = amp4[...].astype(jnp.float32)
+    for l in range(32):
+        osc[pl.ds(l, 4, stride=32), :] = v[:, l * 128 : (l + 1) * 128]
+    amp[pl.ds(spot(c, x, 8), 4)] = osc[0:128, :].reshape(4, 32, 128).astype(jnp.bfloat16)
+    code = dest[...] * 16 + place[...]
+    code = jnp.broadcast_to(jnp.concatenate([code] * 4, axis=1), (8, 128))
+    ca[y * 2 + c] = code
+    cb[x * 2 + c] = code
     pl.semaphore_wait(barrier, len(friends))
 
     def z_send(slot, step):
@@ -127,7 +137,8 @@
         lax.fori_loop(lo // 4, hi // 4, relayout, 0)
         lax.fori_loop(lo, hi, build, 0)
 
-    tiles_in.wait()
+    loads[3].wait()
+    loads[4].wait()
     prep(0, 4)
     z_wait(6)
     z_send(6, 2)
@@ -181,11 +192,13 @@
     z_wait(15)
     x_send(8, 15, 1)
     x_wait(5, 2, 2)
+    k_send(1, 2, 2)
+    x_wait(6, 13, 2)
+    k_send(2, 13, 2)
     x_wait(7, 0, 2)
-    k_send(1, 0, 4)
-    x_wait(6, 13, 2)
+    k_send(3, 0, 2)
     x_wait(8, 15, 1)
-    k_send(2, 13, 3)
+    k_send(4, 15, 1)
     for i in range(4):
         arrived(ca.at[lax.rem(y + 4 - i, 4) * 2 + 1 - c], c_r.at[0, 3 + i], sib)
         arrived(cb.at[lax.rem(x + 4 - i, 4) * 2 + 1 - c], c_r.at[1, 3 + i], sib)
@@ -211,8 +224,10 @@
     sel_b = (spread(cb) == want_b).astype(jnp.bfloat16)
 
     k_wait(0, 4, 9)
-    k_wait(1, 0, 4)
-    k_wait(2, 13, 3)
+    k_wait(1, 2, 2)
+    k_wait(2, 13, 2)
+    k_wait(3, 0, 2)
+    k_wait(4, 15, 1)
 
     def product(q, carry):
         parts = []
@@ -226,24 +241,31 @@
         osc[pl.ds(pl.multiple_of(q * 32, 32), 32), :] = o
         return carry
 
-    lax.fori_loop(0, PAB, product, 0)
-    mine_a = xa.at[y * 2 + c]
-    mine_b = xb.at[x * 2 + c]
-    for r in range(16):
-        mine_a[:, r * 128 : (r + 1) * 128] = osc[pl.ds(r, PAB, stride=32), :].astype(jnp.bfloat16)
-    for i in (1, 2, 3):
-        send(mine_a, mine_a, p_s.at[0, i - 1], p_r.at[0, i - 1], dev(x, y + i, z, c))
-    for r in range(16):
-        mine_b[:, r * 128 : (r + 1) * 128] = osc[pl.ds(16 + r, PAB, stride=32), :].astype(jnp.bfloat16)
-    for i in (1, 2, 3):
-        send(mine_b, mine_b, p_s.at[1, i - 1], p_r.at[1, i - 1], dev(x + i, y, z, c))
-
-    for i in range(4):
-        for h, (ref, me) in enumerate(((xa, y), (xb, x))):
-            s = ref.at[lax.rem(me + 4 - i, 4) * 2 + c]
-            if i > 0:
-                arrived(s, p_r.at[h, i - 1], sib)
-            send(s, s, p_s.at[h, 3 + i], p_r.at[h, 3 + i], sib)
+    def mine(h, j):
+        ref, me = ((xa, y), (xb, x))[h]
+        return lambda i: ref.at[lax.rem(me + 4 - i, 4) * 2 + c, pl.ds(j * 16, 16), :]
+
+    def theirs(h, j, i):
+        ref, me = ((xa, y), (xb, x))[h]
+        return ref.at[lax.rem(me + 4 - i, 4) * 2 + 1 - c, pl.ds(j * 16, 16), :]
+
+    for j in range(2):
+        lax.fori_loop(j * 16, j * 16 + 16, product, 0)
+        for h in range(2):
+            own = mine(h, j)(0)
+            for r in range(16):
+                v = osc[pl.ds(j * 512 + h * 16 + r, 16, stride=32), :]
+                own[:, r * 128 : (r + 1) * 128] = v.astype(jnp.bfloat16)
+            for i in (1, 2, 3):
+                to = dev(x, y + i, z, c) if h == 0 else dev(x + i, y, z, c)
+                send(own, own, p_s.at[h, j, i - 1], p_r.at[h, j, i - 1], to)
+            send(own, own, p_s.at[h, j, 3], p_r.at[h, j, 3], sib)
+    for h in range(2):
+        for j in range(2):
+            for i in (1, 2, 3):
+                got = mine(h, j)(i)
+                arrived(got, p_r.at[h, j, i - 1], sib)
+                send(got, got, p_s.at[h, j, 3 + i], p_r.at[h, j, 3 + i], sib)
 
     def dense(sel, src, dst):
         def chunk(n, carry):
@@ -255,76 +277,89 @@
 
         lax.fori_loop(0, HALF // 256, chunk, 0)
 
-    for i in range(4):
-        arrived(xa.at[lax.rem(y + 4 - i, 4) * 2 + 1 - c], p_r.at[0, 3 + i], sib)
-    dense(sel_a, xa, sa)
-    for i in (1, 2, 3):
-        send(sa.at[lax.rem(x + i, 4)], ra.at[i - 1], q_s.at[0, i - 1], q_r.at[0, i - 1], dev(x + i, y, z, c))
-    for i in range(4):
-        arrived(xb.at[lax.rem(x + 4 - i, 4) * 2 + 1 - c], p_r.at[1, 3 + i], sib)
-    dense(sel_b, xb, sb)
-    for i in (1, 2, 3):
-        send(sb.at[lax.rem(y + i, 4)], rb.at[i - 1], q_s.at[1, i - 1], q_r.at[1, i - 1], dev(x, y + i, z, c))
-
-    def gathered(own, got, dst, at):
+    def exchange(h, sel, src, dst, got):
+        for j in range(2):
+            for i in range(4):
+                arrived(theirs(h, j, i), p_r.at[h, j, 3 + i], sib)
+        dense(sel, src, dst)
+        for i in (1, 2, 3):
+            to = dev(x + i, y, z, c) if h == 0 else dev(x, y + i, z, c)
+            me = x if h == 0 else y
+            send(dst.at[lax.rem(me + i, 4)], got.at[i - 1], q_s.at[h, i - 1], q_r.at[h, i - 1], to)
+
+    exchange(0, sel_a, xa, sa, ra)
+    exchange(1, sel_b, xb, sb, rb)
+
+    b4 = lax.rem(z, 4)
+    a4 = z // 4
+
+    def gathered(h, own, got):
+        for i in (1, 2, 3):
+            arrived(got.at[i - 1], q_r.at[h, i - 1], sib)
+
         def chunk(n, carry):
             lanes = pl.ds(pl.multiple_of(n * 256, 256), 256)
             s = own[:, lanes].astype(jnp.float32)
             for i in range(3):
                 s = s + got[i, :, lanes].astype(jnp.float32)
-            dst[:, :, pl.ds(pl.multiple_of(at + n * 256, 256), 256)] = s.astype(jnp.bfloat16).reshape(4, 16, 256)
+            se[h, :, :, lanes] = s.astype(jnp.bfloat16).reshape(4, 16, 256)
             return carry
 
         lax.fori_loop(0, HALF // 256, chunk, 0)
-
-    for i in (1, 2, 3):
-        arrived(ra.at[i - 1], q_r.at[0, i - 1], sib)
-    gathered(sa.at[x], ra, se, 0)
-    for i in (1, 2, 3):
-        arrived(rb.at[i - 1], q_r.at[1, i - 1], sib)
-    gathered(sb.at[y], rb, se, HALF)
-
-    a4 = z // 4
-    b4 = lax.rem(z, 4)
-    for i in (1, 2, 3):
-        to = lax.rem(b4 + i, 4)
-        send(se.at[to], re.at[i - 1], e_s.at[i - 1], e_r.at[i - 1], dev(x, y, a4 * 4 + to, c))
-    for i in (1, 2, 3):
-        arrived(re.at[i - 1], e_r.at[i - 1], sib)
-    for u in range(4):
-        lanes = slice(u * 1024, (u + 1) * 1024)
-        s = se[b4, :, lanes].astype(jnp.float32)
+        for i, step in enumerate((1, -1, 2 * (2 * h - 1))):
+            to = lax.rem(b4 + step + 4, 4)
+            send(se.at[h, to], re.at[h, i], e_s.at[h, i], e_r.at[h, i], dev(x, y, z + step, c))
+
+    def fours(h):
         for i in range(3):
-            s = s + re[i, :, lanes].astype(jnp.float32)
+            arrived(re.at[h, i], e_r.at[h, i], sib)
+        parts = []
+        for u in range(4):
+            lanes = slice(u * 512, (u + 1) * 512)
+            s = se[h, b4, :, lanes].astype(jnp.float32)
+            for i in range(3):
+                s = s + re[h, i, :, lanes].astype(jnp.float32)
+            parts.append(s)
         for k in range(4):
-            sf[k, u] = s[k * 4 : (k + 1) * 4, :]
-    for i in (1, 2, 3):
-        to = lax.rem(a4 + i, 4)
-        send(sf.at[to], rf.at[i - 1], f_s.at[i - 1], f_r.at[i - 1], dev(x, y, to * 4 + b4, c))
-    for i in (1, 2, 3):
-        arrived(rf.at[i - 1], f_r.at[i - 1], sib)
-    for u in range(4):
-        out_ref[:, u * 1024 : (u + 1) * 1024] = sf[a4, u] + rf[0, u] + rf[1, u] + rf[2, u]
+            v = jnp.concatenate([s[k * 4 : (k + 1) * 4, :] for s in parts], axis=0)
+            sf[h, k] = v.astype(jnp.bfloat16)
+        for i in (1, 2, 3):
+            to = lax.rem(a4 + i, 4)
+            send(sf.at[h, to], rf.at[h, i - 1], f_s.at[h, i - 1], f_r.at[h, i - 1], dev(x, y, z + 4 * i, c))
+
+    def finish(h):
+        s = sf[h, a4].astype(jnp.float32)
+        for i in range(3):
+            arrived(rf.at[h, i], f_r.at[h, i], sib)
+            s = s + rf[h, i].astype(jnp.float32)
+        for u in range(4):
+            at = h * HALF + u * 512
+            out_ref[:, at : at + 512] = s[u * 4 : (u + 1) * 4, :]
+
+    gathered(0, sa.at[x], ra)
+    gathered(1, sb.at[y], rb)
+    fours(0)
+    fours(1)
+    finish(0)
+    finish(1)
 
     for cp in sent:
         cp.wait_send()
 
 
 def per_device(tiles, integral_cd_tile, part_dest, partial_row_place, amplitudes, residual_in):
-    codes = jnp.tile((part_dest[:, 0] * 16 + partial_row_place)[None, :], (8, 4))
-    bf16, f32, dma = jnp.bfloat16, jnp.float32, pltpu.SemaphoreType.DMA
-    vmem = pl.BlockSpec(memory_space=pltpu.VMEM)
+    bf16, f32, i32, dma = jnp.bfloat16, jnp.float32, jnp.int32, pltpu.SemaphoreType.DMA
+    hbm = pl.BlockSpec(memory_space=pltpu.HBM)
     ladder = pl.pallas_call(
         ladder_kernel,
         out_shape=jax.ShapeDtypeStruct((4, 4096), f32),
-        in_specs=[
-            pl.BlockSpec(memory_space=pltpu.SMEM),
-            vmem,
-            vmem,
-            pl.BlockSpec(memory_space=pl.ANY),
-        ],
-        out_specs=vmem,
+        in_specs=[hbm] * 5,
+        out_specs=pl.BlockSpec(memory_space=pltpu.VMEM),
         scratch_shapes=[
+            pltpu.SMEM((128,), i32),
+            pltpu.VMEM((1, 32), i32),
+            pltpu.VMEM((1, 32), i32),
+            pltpu.VMEM((4, 4096), bf16),
             pltpu.VMEM((512, 32, 128), bf16),
             pltpu.VMEM((128, 4096), bf16),
             pltpu.VMEM((4096, 128), f32),
@@ -332,30 +367,36 @@
             pltpu.VMEM((1024, 128), f32),
             pltpu.VMEM((8, 32, HALF), bf16),
             pltpu.VMEM((8, 32, HALF), bf16),
-            pltpu.VMEM((8, 8, 128), jnp.int32),
-            pltpu.VMEM((8, 8, 128), jnp.int32),
+            pltpu.VMEM((8, 8, 128), i32),
+            pltpu.VMEM((8, 8, 128), i32),
             pltpu.VMEM((4, 64, HALF), bf16),
             pltpu.VMEM((4, 64, HALF), bf16),
             pltpu.VMEM((3, 64, HALF), bf16),
             pltpu.VMEM((3, 64, HALF), bf16),
-            pltpu.VMEM((4, 16, 4096), bf16),
-            pltpu.VMEM((3, 16, 4096), bf16),
-            pltpu.VMEM((4, 4, 4, 1024), f32),
-            pltpu.VMEM((3, 4, 4, 1024), f32),
-            dma,
+            pltpu.VMEM((2, 4, 16, HALF), bf16),
+            pltpu.VMEM((2, 3, 16, HALF), bf16),
+            pltpu.VMEM((2, 4, 16, 512), bf16),
+            pltpu.VMEM((2, 3, 16, 512), bf16),
+            dma((5,)),
             dma((16,)), dma((16,)),
             dma((9, 3)), dma((9, 3)),
-            dma((3, 4)), dma((3, 4)),
+            dma((5, 4)), dma((5, 4)),
             dma((2, 7)), dma((2, 7)),
-            dma((2, 7)), dma((2, 7)),
+            dma((2, 2, 7)), dma((2, 2, 7)),
             dma((2, 3)), dma((2, 3)),
-            dma((3,)), dma((3,)),
-            dma((3,)), dma((3,)),
+            dma((2, 3)), dma((2, 3)),
+            dma((2, 3)), dma((2, 3)),
         ],
         compiler_params=pltpu.CompilerParams(
-            collective_id=0, has_side_effects=True, vmem_limit_bytes=48 << 20
+            collective_id=0, has_side_effects=True, vmem_limit_bytes=63 << 20
         ),
-    )(integral_cd_tile, codes, amplitudes.reshape(4, 32, 128), tiles)
+    )(
+        integral_cd_tile,
+        part_dest.reshape(1, PAB),
+        partial_row_place.reshape(1, PAB),
+        amplitudes.reshape(4, 4096),
+        tiles,
+    )
     return residual_in + ladder[None]
 
 

time: 113 us -> 94.3 us (0.83)
  the two profiles are of different devices: /device:TPU:96 before, /device:TPU:6 now
where the time goes in v2:
time: 94.3 us; the launch traced here: 94.1 us
  Pallas kernels  92.5 us (98%)
  other arithmetic  1.49 us (2%)
    pallas_call x1, Pallas kernels, per_device(): pl.pallas_call(ladder_kernel, out_shape=jax.ShapeDtypeStruct((4, 4096), f...  92.5 us

profile of v2, /device:TPU:6, one launch (start us, length us, event | category | flops | bytes accessed | tf_op | source)
XLA Modules:
  0.0 94.1 jit_solution(7641012559185849178)
XLA Ops:
  0.0 0.0 copy-start
  0.0 92.5 %shard_map.64 = f32[4,4096]{1,0:T(4,128)} custom-call(s32[128]{0:T(128)} %cd_hbm.1, s32[1,32]{1,0:T(1,128)} %bitcast.6, s32[1,32]{1,0:T(1,128)} %bitcast.7, bf16[4,4096]{1,0:T(4,128)(2,1)} %bitcast.5, bf16[128,4096]{1,0:T(8,128)(2,1)} %tiles_hbm.1), custom_call_target="tpu_custom_call" | custom-call | tf_op jit(solution)/shard_map/pallas_call | solution.py:353
  92.6 0.0 copy-done
  92.6 1.5 %bitcast_add_fusion = f32[1,4,4096]{2,1,0:T(4,128)} fusion(f32[1,4,4096]{2,1,0:T(4,128)S(1)} %copy-done, f32[4,4096]{1,0:T(4,128)} %shard_map.64), kind=kLoop, calls=%fused_computation | loop fusion | flops 16384 | bytes 196608 | tf_op jit(solution)/shard_map/add | solution.py:400
Async XLA Ops:
  0.0 92.6 %copy-start = (f32[1,4,4096]{2,1,0:T(4,128)S(1)}, f32[1,4,4096]{2,1,0:T(4,128)}, u32[]{:S(2)}) copy-start(f32[1,4,4096]{2,1,0:T(4,128)} %param.11) | copy-start | bytes 196612

commit v3 on v2

--- a/solution.py
+++ b/solution.py
@@ -7,6 +7,7 @@
 
 PAB = 32
 HALF = 2048
+LANES = 1024
 MESH = pl.DeviceIdType.MESH
 
 
@@ -22,7 +23,7 @@
 
 def ladder_kernel(
     cd_hbm, dest_hbm, place_hbm, amp_hbm, tiles_hbm, out_ref,
-    cd_ref, dest, place, amp4, amp, tv, tsc, wbuf, osc, xa, xb, ca, cb, sa, sb, ra, rb, se, re, sf, rf,
+    cd_ref, dest, place, amp4, amp, tv, tsc, wbuf, osc, xa, xb, ca, cb, sd, rd, se, re, sf, rf,
     in_sem, z_s, z_r, x_s, x_r, k_s, k_r, c_s, c_r, p_s, p_r, q_s, q_r, e_s, e_r, f_s, f_r,
 ):
     x, y, z, c = coords()
@@ -42,7 +43,7 @@
 
     sib = dev(x, y, z, c + 1)
     barrier = pltpu.get_barrier_semaphore()
-    friends = [dev(x, y, z + d, c) for d in (1, -1, 2, -2, 4, -4, 8)]
+    friends = [dev(x, y, z + d, c) for d in (1, -1, 2, -2)]
     friends += [dev(x + d, y, z, c) for d in (1, 2, 3)]
     friends += [dev(x, y + d, z, c) for d in (1, 2, 3)]
     friends += [sib]
@@ -250,7 +251,7 @@
         return ref.at[lax.rem(me + 4 - i, 4) * 2 + 1 - c, pl.ds(j * 16, 16), :]
 
     for j in range(2):
-        lax.fori_loop(j * 16, j * 16 + 16, product, 0)
+        lax.fori_loop(j * 16, j * 16 + 16, product, 0, unroll=4)
         for h in range(2):
             own = mine(h, j)(0)
             for r in range(16):
@@ -267,81 +268,77 @@
                 arrived(got, p_r.at[h, j, i - 1], sib)
                 send(got, got, p_s.at[h, j, 3 + i], p_r.at[h, j, 3 + i], sib)
 
-    def dense(sel, src, dst):
-        def chunk(n, carry):
-            lanes = pl.ds(pl.multiple_of(n * 256, 256), 256)
+    def exchange(h, k, sel, src):
+        def part(n, carry):
+            lanes = pl.ds(pl.multiple_of(k * LANES + n * 256, 256), 256)
             v = src[:, :, lanes].reshape(256, 256)
-            s = jnp.dot(sel, v, preferred_element_type=jnp.float32).astype(jnp.bfloat16)
-            dst[:, :, lanes] = s.reshape(4, 64, 256)
+            t = jnp.dot(sel, v, preferred_element_type=jnp.float32).astype(jnp.bfloat16)
+            sd[h, k, :, :, pl.ds(pl.multiple_of(n * 256, 256), 256)] = t.reshape(4, 64, 256)
             return carry
 
-        lax.fori_loop(0, HALF // 256, chunk, 0)
-
-    def exchange(h, sel, src, dst, got):
-        for j in range(2):
-            for i in range(4):
-                arrived(theirs(h, j, i), p_r.at[h, j, 3 + i], sib)
-        dense(sel, src, dst)
+        lax.fori_loop(0, LANES // 256, part, 0, unroll=2)
         for i in (1, 2, 3):
             to = dev(x + i, y, z, c) if h == 0 else dev(x, y + i, z, c)
             me = x if h == 0 else y
-            send(dst.at[lax.rem(me + i, 4)], got.at[i - 1], q_s.at[h, i - 1], q_r.at[h, i - 1], to)
-
-    exchange(0, sel_a, xa, sa, ra)
-    exchange(1, sel_b, xb, sb, rb)
+            send(sd.at[h, k, lax.rem(me + i, 4)], rd.at[h, k, i - 1], q_s.at[h, k, i - 1], q_r.at[h, k, i - 1], to)
 
     b4 = lax.rem(z, 4)
     a4 = z // 4
 
-    def gathered(h, own, got):
-        for i in (1, 2, 3):
-            arrived(got.at[i - 1], q_r.at[h, i - 1], sib)
-
-        def chunk(n, carry):
+    def gathered(h, k):
+        own = x if h == 0 else y
+        for i in range(3):
+            arrived(rd.at[h, k, i], q_r.at[h, k, i], sib)
+
+        def part(n, carry):
             lanes = pl.ds(pl.multiple_of(n * 256, 256), 256)
-            s = own[:, lanes].astype(jnp.float32)
+            t = sd[h, k, own, :, lanes].astype(jnp.float32)
             for i in range(3):
-                s = s + got[i, :, lanes].astype(jnp.float32)
-            se[h, :, :, lanes] = s.astype(jnp.bfloat16).reshape(4, 16, 256)
+                t = t + rd[h, k, i, :, lanes].astype(jnp.float32)
+            se[h, k, :, :, lanes] = t.astype(jnp.bfloat16).reshape(4, 16, 256)
             return carry
 
-        lax.fori_loop(0, HALF // 256, chunk, 0)
+        lax.fori_loop(0, LANES // 256, part, 0)
         for i, step in enumerate((1, -1, 2 * (2 * h - 1))):
             to = lax.rem(b4 + step + 4, 4)
-            send(se.at[h, to], re.at[h, i], e_s.at[h, i], e_r.at[h, i], dev(x, y, z + step, c))
-
-    def fours(h):
+            send(se.at[h, k, to], re.at[h, k, i], e_s.at[h, k, i], e_r.at[h, k, i], dev(x, y, z + step, c))
+
+    def fours(h, k):
         for i in range(3):
-            arrived(re.at[h, i], e_r.at[h, i], sib)
+            arrived(re.at[h, k, i], e_r.at[h, k, i], sib)
         parts = []
         for u in range(4):
-            lanes = slice(u * 512, (u + 1) * 512)
-            s = se[h, b4, :, lanes].astype(jnp.float32)
+            lanes = slice(u * 256, (u + 1) * 256)
+            t = se[h, k, b4, :, lanes].astype(jnp.float32)
             for i in range(3):
-                s = s + re[h, i, :, lanes].astype(jnp.float32)
-            parts.append(s)
-        for k in range(4):
-            v = jnp.concatenate([s[k * 4 : (k + 1) * 4, :] for s in parts], axis=0)
-            sf[h, k] = v.astype(jnp.bfloat16)
+                t = t + re[h, k, i, :, lanes].astype(jnp.float32)
+            parts.append(t)
+        for w in range(4):
+            v = jnp.concatenate([t[w * 4 : (w + 1) * 4, :] for t in parts], axis=0)
+            sf[h, k, w] = v.astype(jnp.bfloat16)
         for i in (1, 2, 3):
             to = lax.rem(a4 + i, 4)
-            send(sf.at[h, to], rf.at[h, i - 1], f_s.at[h, i - 1], f_r.at[h, i - 1], dev(x, y, z + 4 * i, c))
-
-    def finish(h):
-        s = sf[h, a4].astype(jnp.float32)
+            send(sf.at[h, k, to], rf.at[h, k, i - 1], f_s.at[h, k, i - 1], f_r.at[h, k, i - 1], dev(x, y, z + 4 * i, c))
+
+    def finish(h, k):
+        t = sf[h, k, a4].astype(jnp.float32)
         for i in range(3):
-            arrived(rf.at[h, i], f_r.at[h, i], sib)
-            s = s + rf[h, i].astype(jnp.float32)
+            arrived(rf.at[h, k, i], f_r.at[h, k, i], sib)
+            t = t + rf[h, k, i].astype(jnp.float32)
         for u in range(4):
-            at = h * HALF + u * 512
-            out_ref[:, at : at + 512] = s[u * 4 : (u + 1) * 4, :]
-
-    gathered(0, sa.at[x], ra)
-    gathered(1, sb.at[y], rb)
-    fours(0)
-    fours(1)
-    finish(0)
-    finish(1)
+            at = h * HALF + k * LANES + u * 256
+            out_ref[:, at : at + 256] = t[u * 4 : (u + 1) * 4, :]
+
+    chunks = [(h, k) for k in range(2) for h in range(2)]
+    for h, k in chunks:
+        if k == 0:
+            for j in range(2):
+                for i in range(4):
+                    arrived(theirs(h, j, i), p_r.at[h, j, 3 + i], sib)
+        exchange(h, k, (sel_a, sel_b)[h], (xa, xb)[h])
+    for stage in (gathered, fours, finish):
+        for h, k in chunks:
+            stage(h, k)
 
     for cp in sent:
         cp.wait_send()
@@ -369,23 +366,21 @@
             pltpu.VMEM((8, 32, HALF), bf16),
             pltpu.VMEM((8, 8, 128), i32),
             pltpu.VMEM((8, 8, 128), i32),
-            pltpu.VMEM((4, 64, HALF), bf16),
-            pltpu.VMEM((4, 64, HALF), bf16),
-            pltpu.VMEM((3, 64, HALF), bf16),
-            pltpu.VMEM((3, 64, HALF), bf16),
-            pltpu.VMEM((2, 4, 16, HALF), bf16),
-            pltpu.VMEM((2, 3, 16, HALF), bf16),
-            pltpu.VMEM((2, 4, 16, 512), bf16),
-            pltpu.VMEM((2, 3, 16, 512), bf16),
+            pltpu.VMEM((2, 2, 4, 64, LANES), bf16),
+            pltpu.VMEM((2, 2, 3, 64, LANES), bf16),
+            pltpu.VMEM((2, 2, 4, 16, LANES), bf16),
+            pltpu.VMEM((2, 2, 3, 16, LANES), bf16),
+            pltpu.VMEM((2, 2, 4, 16, 256), bf16),
+            pltpu.VMEM((2, 2, 3, 16, 256), bf16),
             dma((5,)),
             dma((16,)), dma((16,)),
             dma((9, 3)), dma((9, 3)),
             dma((5, 4)), dma((5, 4)),
             dma((2, 7)), dma((2, 7)),
             dma((2, 2, 7)), dma((2, 2, 7)),
-            dma((2, 3)), dma((2, 3)),
-            dma((2, 3)), dma((2, 3)),
-            dma((2, 3)), dma((2, 3)),
+            dma((2, 2, 3)), dma((2, 2, 3)),
+            dma((2, 2, 3)), dma((2, 2, 3)),
+            dma((2, 2, 3)), dma((2, 2, 3)),
         ],
         compiler_params=pltpu.CompilerParams(
             collective_id=0, has_side_effects=True, vmem_limit_bytes=63 << 20

time: 94.3 us -> 90 us (0.954)
  Pallas kernels: 92.5 us -> 87.6 us
    pallas_call x1, Pallas kernels: 92.5 us -> 87.6 us  [per_device(): pl.pallas_call(ladder_kernel, out_shape=jax.ShapeDtypeStruct((4, 4096), f...]
where the time goes in v3:
time: 90 us; the launch traced here: 89.1 us
  Pallas kernels  87.6 us (97%)
  other arithmetic  1.49 us (2%)
    pallas_call x1, Pallas kernels, per_device(): pl.pallas_call(ladder_kernel, out_shape=jax.ShapeDtypeStruct((4, 4096), f...  87.6 us

profile of v3, /device:TPU:6, one launch (start us, length us, event | category | flops | bytes accessed | tf_op | source)
XLA Modules:
  0.0 89.1 jit_solution(17699239914313229600)
XLA Ops:
  0.0 0.0 copy-start
  0.0 87.6 %shard_map.64 = f32[4,4096]{1,0:T(4,128)} custom-call(s32[128]{0:T(128)} %cd_hbm.1, s32[1,32]{1,0:T(1,128)} %bitcast.6, s32[1,32]{1,0:T(1,128)} %bitcast.7, bf16[4,4096]{1,0:T(4,128)(2,1)} %bitcast.5, bf16[128,4096]{1,0:T(8,128)(2,1)} %tiles_hbm.1), custom_call_target="tpu_custom_call" | custom-call | tf_op jit(solution)/shard_map/pallas_call | solution.py:350
  87.6 0.0 copy-done
  87.6 1.5 %bitcast_add_fusion = f32[1,4,4096]{2,1,0:T(4,128)} fusion(f32[1,4,4096]{2,1,0:T(4,128)S(1)} %copy-done, f32[4,4096]{1,0:T(4,128)} %shard_map.64), kind=kLoop, calls=%fused_computation | loop fusion | flops 16384 | bytes 196608 | tf_op jit(solution)/shard_map/add | solution.py:395
Async XLA Ops:
  0.0 87.6 %copy-start = (f32[1,4,4096]{2,1,0:T(4,128)S(1)}, f32[1,4,4096]{2,1,0:T(4,128)}, u32[]{:S(2)}) copy-start(f32[1,4,4096]{2,1,0:T(4,128)} %param.11) | copy-start | bytes 196612

commit v4 on v3

--- a/solution.py
+++ b/solution.py
@@ -24,7 +24,7 @@
 def ladder_kernel(
     cd_hbm, dest_hbm, place_hbm, amp_hbm, tiles_hbm, out_ref,
     cd_ref, dest, place, amp4, amp, tv, tsc, wbuf, osc, xa, xb, ca, cb, sd, rd, se, re, sf, rf,
-    in_sem, z_s, z_r, x_s, x_r, k_s, k_r, c_s, c_r, p_s, p_r, q_s, q_r, e_s, e_r, f_s, f_r,
+    in_sem, z_s, z_r, o_s, o_r, g_s, g_r, x_s, x_r, k_s, k_r, c_s, c_r, p_s, p_r, q_s, q_r, e_s, e_r, f_s, f_r,
 ):
     x, y, z, c = coords()
     sent = []
@@ -56,30 +56,45 @@
         loads.append(pltpu.make_async_copy(src, dst, in_sem.at[i]))
         loads[-1].start()
 
-    def spot(cc, xx, slot):
-        return pl.multiple_of(((cc * 4 + xx) * 16 + slot) * 4, 4)
-
     def block(xx, slot, n=1, cc=None):
-        return amp.at[pl.ds(spot(c if cc is None else cc, xx, slot), 4 * n)]
+        cc = c if cc is None else cc
+        return amp.at[pl.ds(((cc * 4 + xx) * 16 + slot) * 3, 3 * n)]
+
+    def first(slot, n=1, cc=None):
+        cc = c if cc is None else cc
+        return amp.at[pl.ds(384 + (cc * 16 + slot) * 4, 4 * n)]
 
     for i in range(3):
         loads[i].wait()
     v = amp4[...].astype(jnp.float32)
     for l in range(32):
         osc[pl.ds(l, 4, stride=32), :] = v[:, l * 128 : (l + 1) * 128]
-    amp[pl.ds(spot(c, x, 8), 4)] = osc[0:128, :].reshape(4, 32, 128).astype(jnp.bfloat16)
+    v = osc[0:128, :].reshape(4, 32, 128).astype(jnp.bfloat16)
+    one = 384 + (c * 16 + 8) * 4 + x
+    amp[one] = v[0]
+    amp[pl.ds(((c * 4 + x) * 16 + 8) * 3, 3)] = v[1:4]
     code = dest[...] * 16 + place[...]
     code = jnp.broadcast_to(jnp.concatenate([code] * 4, axis=1), (8, 128))
     ca[y * 2 + c] = code
     cb[x * 2 + c] = code
     pl.semaphore_wait(barrier, len(friends))
 
-    def z_send(slot, step):
-        nslot = slot - step
-        send(block(x, slot), block(x, nslot), z_s.at[nslot], z_r.at[nslot], dev(x, y, z + step, c))
-
-    def z_wait(slot):
-        arrived(block(x, slot), z_r.at[slot], sib)
+    def z_send(kind, slot, step):
+        to = slot - step
+        src, dst = (first(slot), first(to)) if kind else (block(x, slot), block(x, to))
+        send(src, dst, z_s.at[kind, to], z_r.at[kind, to], dev(x, y, z + step, c))
+
+    def z_wait(kind, slot):
+        arrived(first(slot) if kind else block(x, slot), z_r.at[kind, slot], sib)
+
+    def z_relay(kind, left, right):
+        z_wait(kind, left)
+        z_send(kind, left, 2)
+        z_send(kind, left, 1)
+        z_wait(kind, right)
+        if right < 14:
+            z_send(kind, right, -2)
+        z_send(kind, right, -1)
 
     def x_send(g, slot, n):
         for i in (1, 2, 3):
@@ -99,8 +114,16 @@
             xs = lax.rem(x + 4 - i, 4)
             arrived(block(xs, slot, n, 1 - c), k_r.at[g, i], sib)
 
+    def f_send(g, slot, n):
+        send(first(slot, n), first(slot, n), g_s.at[g], g_r.at[g], sib)
+
+    def f_wait(g, slot, n):
+        arrived(first(slot, n, 1 - c), g_r.at[g], sib)
+
+    for i in (1, 2, 3):
+        send(amp.at[one], amp.at[one], o_s.at[i - 1], o_r.at[i - 1], dev(x + i, y, z, c))
     for step in (2, -2, 1, -1):
-        z_send(8, step)
+        z_send(0, 8, step)
     x_send(0, 8, 1)
     for i in (1, 2, 3):
         me = ca.at[y * 2 + c]
@@ -141,57 +164,66 @@
     loads[3].wait()
     loads[4].wait()
     prep(0, 4)
-    z_wait(6)
-    z_send(6, 2)
-    z_send(6, 1)
-    z_wait(10)
-    z_send(10, -2)
-    z_send(10, -1)
-    z_wait(7)
+    for i in (1, 2, 3):
+        got = amp.at[384 + (c * 16 + 8) * 4 + lax.rem(x + 4 - i, 4)]
+        arrived(got, o_r.at[i - 1], sib)
+    for step in (2, -2, 1, -1):
+        z_send(1, 8, step)
+    z_relay(0, 6, 10)
+    z_wait(0, 7)
     x_send(1, 6, 2)
-    z_wait(9)
+    z_wait(0, 9)
     x_send(2, 9, 2)
     prep(4, 8)
-    z_wait(4)
-    z_send(4, 2)
-    z_send(4, 1)
-    z_wait(12)
-    z_send(12, -2)
-    z_send(12, -1)
-    z_wait(5)
+    z_relay(1, 6, 10)
+    prep(8, 12)
+    z_relay(0, 4, 12)
+    z_wait(0, 5)
     x_send(3, 4, 2)
-    z_wait(11)
+    z_wait(0, 11)
     x_send(4, 11, 2)
-    prep(8, 16)
-    z_wait(2)
-    z_send(2, 2)
-    z_send(2, 1)
-    z_wait(14)
-    z_send(14, -1)
-    z_wait(3)
+    prep(12, 16)
+    z_relay(1, 4, 12)
+    prep(16, 20)
+    z_relay(0, 2, 14)
+    z_wait(0, 3)
     x_send(5, 2, 2)
-    z_wait(13)
+    z_wait(0, 13)
     x_send(6, 13, 2)
+    prep(20, 24)
+    z_relay(1, 2, 14)
+    for i in (1, 2, 3):
+        arrived(ca.at[lax.rem(y + 4 - i, 4) * 2 + c], c_r.at[0, i - 1], sib)
+        arrived(cb.at[lax.rem(x + 4 - i, 4) * 2 + c], c_r.at[1, i - 1], sib)
+    for i in range(4):
+        t = ca.at[lax.rem(y + 4 - i, 4) * 2 + c]
+        send(t, t, c_s.at[0, 3 + i], c_r.at[0, 3 + i], sib)
+        t = cb.at[lax.rem(x + 4 - i, 4) * 2 + c]
+        send(t, t, c_s.at[1, 3 + i], c_r.at[1, 3 + i], sib)
+    z_wait(0, 0)
+    z_wait(0, 1)
+    x_send(7, 0, 2)
+    z_wait(0, 15)
+    x_send(8, 15, 1)
+    prep(24, 32)
+    for slot in (5, 7, 9, 11):
+        z_wait(1, slot)
+    f_send(0, 4, 9)
     x_wait(0, 8, 1)
     x_wait(1, 6, 2)
     x_wait(2, 9, 2)
     x_wait(3, 4, 2)
     x_wait(4, 11, 2)
     k_send(0, 4, 9)
-    for i in (1, 2, 3):
-        arrived(ca.at[lax.rem(y + 4 - i, 4) * 2 + c], c_r.at[0, i - 1], sib)
-        arrived(cb.at[lax.rem(x + 4 - i, 4) * 2 + c], c_r.at[1, i - 1], sib)
-    for i in range(4):
-        s = ca.at[lax.rem(y + 4 - i, 4) * 2 + c]
-        send(s, s, c_s.at[0, 3 + i], c_r.at[0, 3 + i], sib)
-        s = cb.at[lax.rem(x + 4 - i, 4) * 2 + c]
-        send(s, s, c_s.at[1, 3 + i], c_r.at[1, 3 + i], sib)
-    prep(16, 32)
-    z_wait(0)
-    z_wait(1)
-    x_send(7, 0, 2)
-    z_wait(15)
-    x_send(8, 15, 1)
+    z_wait(1, 3)
+    f_send(1, 2, 2)
+    z_wait(1, 13)
+    f_send(2, 13, 2)
+    z_wait(1, 0)
+    z_wait(1, 1)
+    f_send(3, 0, 2)
+    z_wait(1, 15)
+    f_send(4, 15, 1)
     x_wait(5, 2, 2)
     k_send(1, 2, 2)
     x_wait(6, 13, 2)
@@ -224,11 +256,9 @@
     want_b = ((x * 16 + zz) * 2 + c) * 16 + other * 4 + p
     sel_b = (spread(cb) == want_b).astype(jnp.bfloat16)
 
-    k_wait(0, 4, 9)
-    k_wait(1, 2, 2)
-    k_wait(2, 13, 2)
-    k_wait(3, 0, 2)
-    k_wait(4, 15, 1)
+    for g, slot, n in ((0, 4, 9), (1, 2, 2), (2, 13, 2), (3, 0, 2), (4, 15, 1)):
+        f_wait(g, slot, n)
+        k_wait(g, slot, n)
 
     def product(q, carry):
         parts = []
@@ -236,7 +266,9 @@
             cd = cd_ref[q * 4 + t]
             hr = cd // 4
             slot = lax.rem(lax.rem(hr // 2, 16) - z + 24, 16)
-            parts.append(amp[((lax.rem(hr, 2) * 4 + hr // 32) * 16 + slot) * 4 + lax.rem(cd, 4)])
+            xx, cc, at = hr // 32, lax.rem(hr, 2), lax.rem(cd, 4)
+            three = ((cc * 4 + xx) * 16 + slot) * 3 + at - 1
+            parts.append(amp[jnp.where(at == 0, 384 + (cc * 16 + slot) * 4 + xx, three)])
         a = jnp.concatenate(parts, axis=1)
         o = lax.dot_general(a, wbuf[q], (((1,), (1,)), ((), ())), preferred_element_type=jnp.float32)
         osc[pl.ds(pl.multiple_of(q * 32, 32), 32), :] = o
@@ -373,7 +405,9 @@
             pltpu.VMEM((2, 2, 4, 16, 256), bf16),
             pltpu.VMEM((2, 2, 3, 16, 256), bf16),
             dma((5,)),
-            dma((16,)), dma((16,)),
+            dma((2, 16)), dma((2, 16)),
+            dma((3,)), dma((3,)),
+            dma((5,)), dma((5,)),
             dma((9, 3)), dma((9, 3)),
             dma((5, 4)), dma((5, 4)),
             dma((2, 7)), dma((2, 7)),

time: 90 us -> 82.9 us (0.921)
  Pallas kernels: 87.6 us -> 81.2 us
    pallas_call x1, Pallas kernels: 87.6 us -> 81.2 us  [per_device(): pl.pallas_call(ladder_kernel, out_shape=jax.ShapeDtypeStruct((4, 4096), f...]
where the time goes in v4:
time: 82.9 us; the launch traced here: 82.7 us
  Pallas kernels  81.2 us (98%)
  other arithmetic  1.49 us (2%)
    pallas_call x1, Pallas kernels, per_device(): pl.pallas_call(ladder_kernel, out_shape=jax.ShapeDtypeStruct((4, 4096), f...  81.2 us

profile of v4, /device:TPU:6, one launch (start us, length us, event | category | flops | bytes accessed | tf_op | source)
XLA Modules:
  0.0 82.7 jit_solution(11553806812347680741)
XLA Ops:
  0.0 0.0 copy-start
  0.0 81.2 %shard_map.64 = f32[4,4096]{1,0:T(4,128)} custom-call(s32[128]{0:T(128)} %cd_hbm.1, s32[1,32]{1,0:T(1,128)} %bitcast.6, s32[1,32]{1,0:T(1,128)} %bitcast.7, bf16[4,4096]{1,0:T(4,128)(2,1)} %bitcast.5, bf16[128,4096]{1,0:T(8,128)(2,1)} %tiles_hbm.1), custom_call_target="tpu_custom_call" | custom-call | tf_op jit(solution)/shard_map/pallas_call | solution.py:382
  81.2 0.0 copy-done
  81.2 1.5 %bitcast_add_fusion = f32[1,4,4096]{2,1,0:T(4,128)} fusion(f32[1,4,4096]{2,1,0:T(4,128)S(1)} %copy-done, f32[4,4096]{1,0:T(4,128)} %shard_map.64), kind=kLoop, calls=%fused_computation | loop fusion | flops 16384 | bytes 196608 | tf_op jit(solution)/shard_map/add | solution.py:429
Async XLA Ops:
  0.0 81.2 %copy-start = (f32[1,4,4096]{2,1,0:T(4,128)S(1)}, f32[1,4,4096]{2,1,0:T(4,128)}, u32[]{:S(2)}) copy-start(f32[1,4,4096]{2,1,0:T(4,128)} %param.11) | copy-start | bytes 196612

commit v5 on v4

--- a/solution.py
+++ b/solution.py
@@ -23,7 +23,7 @@
 
 def ladder_kernel(
     cd_hbm, dest_hbm, place_hbm, amp_hbm, tiles_hbm, out_ref,
-    cd_ref, dest, place, amp4, amp, tv, tsc, wbuf, osc, xa, xb, ca, cb, sd, rd, se, re, sf, rf,
+    cd_ref, dest, place, amp4, amp, tv, tsc, wbuf, osc, xa, xb, ca, cb, sd, rd, se, re, kept, sf, rf,
     in_sem, z_s, z_r, o_s, o_r, g_s, g_r, x_s, x_r, k_s, k_r, c_s, c_r, p_s, p_r, q_s, q_r, e_s, e_r, f_s, f_r,
 ):
     x, y, z, c = coords()
@@ -100,14 +100,12 @@
         for i in (1, 2, 3):
             send(block(x, slot, n), block(x, slot, n), x_s.at[g, i - 1], x_r.at[g, i - 1], dev(x + i, y, z, c))
 
-    def x_wait(g, slot, n):
-        for i in (1, 2, 3):
-            arrived(block(lax.rem(x + 4 - i, 4), slot, n), x_r.at[g, i - 1], sib)
-
-    def k_send(g, slot, n):
-        for i in range(4):
-            xs = lax.rem(x + 4 - i, 4)
-            send(block(xs, slot, n), block(xs, slot, n), k_s.at[g, i], k_r.at[g, i], sib)
+    def k_send(g, slot, n, i, wait=()):
+        xs = lax.rem(x + 4 - i, 4)
+        if i > 0:
+            for w, ws, wn in wait:
+                arrived(block(xs, ws, wn), x_r.at[w, i - 1], sib)
+        send(block(xs, slot, n), block(xs, slot, n), k_s.at[g, i], k_r.at[g, i], sib)
 
     def k_wait(g, slot, n):
         for i in range(4):
@@ -159,7 +157,7 @@
 
     def prep(lo, hi):
         lax.fori_loop(lo // 4, hi // 4, relayout, 0)
-        lax.fori_loop(lo, hi, build, 0)
+        lax.fori_loop(lo, hi, build, 0, unroll=4)
 
     loads[3].wait()
     loads[4].wait()
@@ -209,12 +207,10 @@
     for slot in (5, 7, 9, 11):
         z_wait(1, slot)
     f_send(0, 4, 9)
-    x_wait(0, 8, 1)
-    x_wait(1, 6, 2)
-    x_wait(2, 9, 2)
-    x_wait(3, 4, 2)
-    x_wait(4, 11, 2)
-    k_send(0, 4, 9)
+    for i in (0, 1, 3, 2):
+        k_send(0, 4, 9, i, ((0, 8, 1), (1, 6, 2), (2, 9, 2), (3, 4, 2), (4, 11, 2)))
+    for g, slot, n in ((1, 2, 2), (2, 13, 2), (3, 0, 2), (4, 15, 1)):
+        k_send(g, slot, n, 0)
     z_wait(1, 3)
     f_send(1, 2, 2)
     z_wait(1, 13)
@@ -224,14 +220,9 @@
     f_send(3, 0, 2)
     z_wait(1, 15)
     f_send(4, 15, 1)
-    x_wait(5, 2, 2)
-    k_send(1, 2, 2)
-    x_wait(6, 13, 2)
-    k_send(2, 13, 2)
-    x_wait(7, 0, 2)
-    k_send(3, 0, 2)
-    x_wait(8, 15, 1)
-    k_send(4, 15, 1)
+    for g, slot, n in ((1, 2, 2), (2, 13, 2), (3, 0, 2), (4, 15, 1)):
+        for i in (1, 3, 2):
+            k_send(g, slot, n, i, ((g + 4, slot, n),))
     for i in range(4):
         arrived(ca.at[lax.rem(y + 4 - i, 4) * 2 + 1 - c], c_r.at[0, 3 + i], sib)
         arrived(cb.at[lax.rem(x + 4 - i, 4) * 2 + 1 - c], c_r.at[1, 3 + i], sib)
@@ -283,7 +274,7 @@
         return ref.at[lax.rem(me + 4 - i, 4) * 2 + 1 - c, pl.ds(j * 16, 16), :]
 
     for j in range(2):
-        lax.fori_loop(j * 16, j * 16 + 16, product, 0, unroll=4)
+        lax.fori_loop(j * 16, j * 16 + 16, product, 0, unroll=16)
         for h in range(2):
             own = mine(h, j)(0)
             for r in range(16):
@@ -293,9 +284,9 @@
                 to = dev(x, y + i, z, c) if h == 0 else dev(x + i, y, z, c)
                 send(own, own, p_s.at[h, j, i - 1], p_r.at[h, j, i - 1], to)
             send(own, own, p_s.at[h, j, 3], p_r.at[h, j, 3], sib)
-    for h in range(2):
-        for j in range(2):
-            for i in (1, 2, 3):
+    for j in range(2):
+        for i in (1, 3, 2):
+            for h in range(2):
                 got = mine(h, j)(i)
                 arrived(got, p_r.at[h, j, i - 1], sib)
                 send(got, got, p_s.at[h, j, 3 + i], p_r.at[h, j, 3 + i], sib)
@@ -327,10 +318,12 @@
             t = sd[h, k, own, :, lanes].astype(jnp.float32)
             for i in range(3):
                 t = t + rd[h, k, i, :, lanes].astype(jnp.float32)
-            se[h, k, :, :, lanes] = t.astype(jnp.bfloat16).reshape(4, 16, 256)
+            t = t.reshape(4, 16, 256)
+            kept[h, k, :, :, lanes] = t
+            se[h, k, :, :, lanes] = t.astype(jnp.bfloat16)
             return carry
 
-        lax.fori_loop(0, LANES // 256, part, 0)
+        lax.fori_loop(0, LANES // 256, part, 0, unroll=2)
         for i, step in enumerate((1, -1, 2 * (2 * h - 1))):
             to = lax.rem(b4 + step + 4, 4)
             send(se.at[h, k, to], re.at[h, k, i], e_s.at[h, k, i], e_r.at[h, k, i], dev(x, y, z + step, c))
@@ -341,22 +334,22 @@
         parts = []
         for u in range(4):
             lanes = slice(u * 256, (u + 1) * 256)
-            t = se[h, k, b4, :, lanes].astype(jnp.float32)
+            t = kept[h, k, b4, :, lanes]
             for i in range(3):
                 t = t + re[h, k, i, :, lanes].astype(jnp.float32)
             parts.append(t)
         for w in range(4):
             v = jnp.concatenate([t[w * 4 : (w + 1) * 4, :] for t in parts], axis=0)
-            sf[h, k, w] = v.astype(jnp.bfloat16)
+            sf[h, k, w] = v
         for i in (1, 2, 3):
             to = lax.rem(a4 + i, 4)
             send(sf.at[h, k, to], rf.at[h, k, i - 1], f_s.at[h, k, i - 1], f_r.at[h, k, i - 1], dev(x, y, z + 4 * i, c))
 
     def finish(h, k):
-        t = sf[h, k, a4].astype(jnp.float32)
+        t = sf[h, k, a4]
         for i in range(3):
             arrived(rf.at[h, k, i], f_r.at[h, k, i], sib)
-            t = t + rf[h, k, i].astype(jnp.float32)
+            t = t + rf[h, k, i]
         for u in range(4):
             at = h * HALF + k * LANES + u * 256
             out_ref[:, at : at + 256] = t[u * 4 : (u + 1) * 4, :]
@@ -402,8 +395,9 @@
             pltpu.VMEM((2, 2, 3, 64, LANES), bf16),
             pltpu.VMEM((2, 2, 4, 16, LANES), bf16),
             pltpu.VMEM((2, 2, 3, 16, LANES), bf16),
-            pltpu.VMEM((2, 2, 4, 16, 256), bf16),
-            pltpu.VMEM((2, 2, 3, 16, 256), bf16),
+            pltpu.VMEM((2, 2, 4, 16, LANES), f32),
+            pltpu.VMEM((2, 2, 4, 16, 256), f32),
+            pltpu.VMEM((2, 2, 3, 16, 256), f32),
             dma((5,)),
             dma((2, 16)), dma((2, 16)),
             dma((3,)), dma((3,)),

time: 82.9 us -> 86.1 us (1.039); the launches traced: 82.7 us -> 84.7 us
  Pallas kernels: 81.2 us -> 83.2 us
    pallas_call x1, Pallas kernels: 81.2 us -> 83.2 us  [per_device(): pl.pallas_call(ladder_kernel, out_shape=jax.ShapeDtypeStruct((4, 4096), f...]
where the time goes in v5:
time: 86.1 us; the launch traced here: 84.7 us
  Pallas kernels  83.2 us (97%)
  other arithmetic  1.49 us (2%)
    pallas_call x1, Pallas kernels, per_device(): pl.pallas_call(ladder_kernel, out_shape=jax.ShapeDtypeStruct((4, 4096), f...  83.2 us

profile of v5, /device:TPU:6, one launch (start us, length us, event | category | flops | bytes accessed | tf_op | source)
XLA Modules:
  0.0 84.7 jit_solution(15230010436036622961)
XLA Ops:
  0.0 0.0 copy-start
  0.0 83.2 %shard_map.64 = f32[4,4096]{1,0:T(4,128)} custom-call(s32[128]{0:T(128)} %cd_hbm.1, s32[1,32]{1,0:T(1,128)} %bitcast.6, s32[1,32]{1,0:T(1,128)} %bitcast.7, bf16[4,4096]{1,0:T(4,128)(2,1)} %bitcast.5, bf16[128,4096]{1,0:T(8,128)(2,1)} %tiles_hbm.1), custom_call_target="tpu_custom_call" | custom-call | tf_op jit(solution)/shard_map/pallas_call | solution.py:375
  83.2 0.0 copy-done
  83.2 1.5 %bitcast_add_fusion = f32[1,4,4096]{2,1,0:T(4,128)} fusion(f32[1,4,4096]{2,1,0:T(4,128)S(1)} %copy-done, f32[4,4096]{1,0:T(4,128)} %shard_map.64), kind=kLoop, calls=%fused_computation | loop fusion | flops 16384 | bytes 196608 | tf_op jit(solution)/shard_map/add | solution.py:423
Async XLA Ops:
  0.0 83.2 %copy-start = (f32[1,4,4096]{2,1,0:T(4,128)S(1)}, f32[1,4,4096]{2,1,0:T(4,128)}, u32[]{:S(2)}) copy-start(f32[1,4,4096]{2,1,0:T(4,128)} %param.11) | copy-start | bytes 196612
